TPU v7x, 32 devices: a whole 2x2x4 slice. The times are simulated.
32 devices in a mesh: groups: 2 (over y), dp: 4 (over z), mp: 4 (over x, core).
Axes of the slice: x: 2, y: 2, z: 4, core: 2. Of those that a mesh axis runs over, the one named last changes fastest.
Arguments:
- qkv_home: bfloat16 [8, 764, 3, 3072], P(('groups', 'dp'), None, None, 'mp'), parts along dimension 0, may hold values from -6 to 6
- resid_home: bfloat16 [8, 764, 6144], P(('groups', 'dp'), None, 'mp'), parts along dimension 0, may hold values from -6 to 6
- out_weight: bfloat16 [3072, 6144], P('dp', 'mp'), may hold values from -0.109375 to 0.109375
- label_weight: bfloat16 [6144, 12288], P('mp', 'dp'), may hold values from -0.21875 to 0.21875
- label_bias: float32 [12288], P('dp'), may hold values from -5 to 5
- query_gain: float32 [128], replicated, may hold values from 0.25 to 1.75
- key_gain: float32 [128], replicated, may hold values from 0.25 to 1.75
- patch_counts: int32 [8, 4], P('groups'), parts along dimension 0, may hold values from 1 to 191, as said below
- move_plan: int32 [8, 4], P('groups'), parts along dimension 0, may hold values from 0 to 3, as said below
- segment_ids: int32 [8, 764], P(('groups', 'dp')), parts along dimension 0, may hold values from 0 to 4, as said below
Outputs:
- mixed: bfloat16 [8, 384, 6144], P(('groups', 'dp'), None, 'mp'), parts along dimension 0
- labels: float32 [8, 4, 12288], P(('groups', 'dp'), 'mp'), parts along dimension 0
There are 2 independent parts, one for each index of `groups`. A program takes and returns all parts, laid end to end along the dimension named above; an argument that names none is the same for every part. Nothing has to cross between parts.
Inputs may be any that keep to these rules, and one draw needn't show every extreme that they name: `patch_counts`: home row r holds its 4 images packed in the order j; every destination row receives exactly one image from every home row, 384 patches in all; every draw holds an image of 191 patches. Every row of move_plan is a permutation, and every destination row appears once in every column, so each destination receives one image from each home row. `segment_ids`: image j of home row r has id j on its patch_counts[r, j] slots, which follow those of image j - 1; slots after the last image have id 4.
All inputs are finite; a program needn't handle non-finite values.
Results may differ from a plain program's by a relative error of at most 0.0065.
Values may be sent and summed in bfloat16 or wider, within the bound.
A program may use at most 64 MiB of HBM per device.

v0:
```python
import math
import jax
import jax.numpy as jnp
from jax import lax
from jax.sharding import PartitionSpec as P

TOK = 384
EPSILON = 1e-06


def head_norm(values, norm_gain):
    center = values - jnp.mean(values, axis=-1, keepdims=True)
    spread = jnp.mean(center * center, axis=-1, keepdims=True)
    return center * lax.rsqrt(spread + EPSILON) * norm_gain


def attend(qkv_rows, seg_rows, query_gain, key_gain):
    length = qkv_rows.shape[0]
    head_width = query_gain.shape[0]
    head_count = qkv_rows.shape[2] // head_width
    split_parts = qkv_rows.reshape(length, 3, head_count, head_width)
    queries = head_norm(split_parts[:, 0].astype(jnp.float32), query_gain).astype(jnp.bfloat16)
    key_rows = head_norm(split_parts[:, 1].astype(jnp.float32), key_gain).astype(jnp.bfloat16)
    scores = jnp.einsum(
        "qhd,khd->hqk", queries, key_rows, preferred_element_type=jnp.float32
    ) / math.sqrt(head_width)
    same_image = seg_rows[:, None] == seg_rows[None, :]
    raised = jnp.where(same_image[None], jnp.exp(scores), 0.0)
    weights = (raised / jnp.sum(raised, axis=-1, keepdims=True)).astype(jnp.bfloat16)
    head_out = jnp.einsum(
        "hqk,khd->qhd", weights, split_parts[:, 2], preferred_element_type=jnp.float32
    )
    return head_out.reshape(length, head_count * head_width).astype(jnp.bfloat16)


def project(heads_local, resid_rows, out_weight):
    gathered = lax.all_gather(heads_local, "mp", axis=1, tiled=True)
    running = resid_rows.astype(jnp.float32) + jnp.dot(
        gathered,
        lax.all_gather(out_weight, "dp", axis=0, tiled=True),
        preferred_element_type=jnp.float32,
    )
    return running.astype(jnp.bfloat16)


def pool(row_mixed, seg_rows, count_row):
    images = count_row.shape[0]
    member_ids = lax.broadcasted_iota(jnp.int32, (images, seg_rows.shape[0]), 0)
    member = (member_ids == seg_rows[None, :]).astype(jnp.bfloat16)
    image_sums = jnp.dot(member, row_mixed, preferred_element_type=jnp.float32)
    return (image_sums / count_row[:, None].astype(jnp.float32)).astype(jnp.bfloat16)


def label_terms(pooled, label_weight):
    return jnp.einsum(
        "abd,dc->abc",
        lax.all_gather(pooled[None], "dp", axis=0, tiled=True),
        label_weight,
        preferred_element_type=jnp.float32,
    )


def pick(values, row_index, is_valid):
    taken = jnp.take(values, row_index, axis=0)
    taken = taken.reshape(is_valid.shape + values.shape[1:])
    keep_mask = is_valid.reshape(is_valid.shape + (1,) * (values.ndim - 1))
    return jnp.where(keep_mask, taken, jnp.zeros_like(taken))


def on_device(
    qkv_home,
    resid_home,
    out_weight,
    label_weight,
    label_bias,
    query_gain,
    key_gain,
    patch_counts,
    move_plan,
    segment_ids,
):
    row_count = lax.axis_size("dp")
    my_index = lax.axis_index("dp")
    home_slots = segment_ids.shape[1]
    pair_slots = home_slots // row_count
    image_ids = lax.broadcasted_iota(jnp.int32, (row_count, row_count, row_count), 2)
    image_ends = jnp.cumsum(patch_counts, axis=1)
    starts = image_ends - patch_counts
    matches = (move_plan[:, :, None] == image_ids).astype(jnp.int32)
    image_sizes = jnp.sum(patch_counts[:, :, None] * matches, axis=1)
    firsts = jnp.sum(starts[:, :, None] * matches, axis=1)
    send_sizes = lax.dynamic_index_in_dim(image_sizes, my_index, 0, keepdims=False)
    send_firsts = lax.dynamic_index_in_dim(firsts, my_index, 0, keepdims=False)
    within = lax.broadcasted_iota(jnp.int32, (row_count, pair_slots), 1)
    send_valid = within < send_sizes[:, None]
    send_index = jnp.minimum(send_firsts[:, None] + within, home_slots - 1).reshape(-1)
    arrive_sizes = lax.dynamic_index_in_dim(image_sizes, my_index, 1, keepdims=False)
    arrive_ends = jnp.cumsum(arrive_sizes)
    arrive_starts = arrive_ends - arrive_sizes
    slot_grid = lax.broadcasted_iota(jnp.int32, (TOK, row_count), 0)
    source = jnp.sum((slot_grid >= arrive_ends[None, :]).astype(jnp.int32), axis=1)
    chosen = (source[:, None] == lax.broadcasted_iota(jnp.int32, (TOK, row_count), 1)).astype(
        jnp.int32
    )
    arrive_index = (
        source * pair_slots + slot_grid[:, 0] - jnp.sum(chosen * arrive_starts[None, :], axis=1)
    )
    home_mixed = project(
        attend(qkv_home[0], segment_ids[0], query_gain, key_gain), resid_home[0], out_weight
    )
    count_row = lax.dynamic_index_in_dim(patch_counts, my_index, 0, keepdims=False)
    pooled = pool(home_mixed, segment_ids[0], count_row)
    partial_value = label_terms(pooled, label_weight)
    send_mixed = pick(home_mixed, send_index, send_valid)
    got_mixed = lax.all_to_all(send_mixed, "dp", split_axis=0, concat_axis=0, tiled=True)
    mixed = jnp.take(got_mixed.reshape(row_count * pair_slots, -1), arrive_index, axis=0)
    logit_sums = lax.psum_scatter(
        partial_value.astype(jnp.bfloat16), "mp", scatter_dimension=1, tiled=True
    ).astype(jnp.float32)
    class_probs = jax.nn.sigmoid(logit_sums + label_bias[None, None, :])
    labels = lax.all_to_all(
        class_probs.astype(jnp.bfloat16), "dp", split_axis=0, concat_axis=2, tiled=True
    ).astype(class_probs.dtype)
    return (mixed[None], labels)


def solution(mesh):
    return jax.shard_map(
        on_device,
        mesh=mesh,
        in_specs=(
            P(("groups", "dp"), None, None, "mp"),
            P(("groups", "dp"), None, "mp"),
            P("dp", "mp"),
            P("mp", "dp"),
            P("dp"),
            P(),
            P(),
            P("groups", None),
            P("groups", None),
            P(("groups", "dp"), None),
        ),
        out_specs=(P(("groups", "dp"), None, "mp"), P(("groups", "dp"), "mp", None)),
        check_vma=False,
    )
```

profile of v0, /device:TPU:0, one launch (start us, length us, event | category | flops | bytes accessed | tf_op | source)
XLA Modules:
  0.0 383.3 jit_solution(16641087347745729092)
XLA Ops:
  7.2 0.0 all-gather.5.cloned.1.call-start
  7.2 4.3 %copy.31 = bf16[1,764,3,768]{1,3,2,0:T(8,128)(2,1)S(1)} copy(bf16[1,764,3,768]{3,1,2,0:T(8,128)(2,1)} %param.10) | data formatting | bytes 7041024 | tf_op args[0]
  11.5 0.0 copy-start.5
  11.5 0.0 copy-start.7
  11.5 0.0 copy-start.8
  11.5 0.4 convert_reduce_fusion.1
  11.9 0.0 copy-start.1
  12.0 0.0 copy-start.2
  12.0 0.7 fusion.11
  12.7 0.6 add_rsqrt_fusion
  13.3 0.0 copy-done.1
  13.3 0.0 copy-done.2
  13.3 0.6 add_rsqrt_fusion.1
  13.9 0.0 copy-done.5
  13.9 0.4 broadcast_compare_fusion
  14.3 0.0 copy-done.7
  14.3 0.0 copy-done.8
  14.4 0.0 copy-start
  14.4 8.7 %fusion = (f32[6,764]{1,0:T(8,128)}, f32[6,764,764]{1,2,0:T(8,128)}) fusion(pred[764,764]{0,1:T(8,128)(4,1)S(1)} %broadcast_compare_fusion, f32[128]{0:T(128)S(1)} %copy-done.7, f32[764,6]{0,1:T(8,128)} %add_rsqrt_fusion, f32[764,6]{0,1:T(8,128)} %copy-done.1, bf16[764,3,6,128]{0,3,2,1:T(8,128)(2,1)S(1)} %bitcast.68, f32[128]{0:T(128)S(1)} %copy-done.8, ...), kind=kOutput, calls=%fused_computation.4 | convolution fusion | flops 912926592 | bytes 17050528 | tf_op jit(solution)/shard_map/qhd,khd->hqk/dot_general | solution.py:24
  23.0 0.0 copy-done
  23.0 8.3 %fusion.22 = bf16[6,764,128]{1,2,0:T(8,128)(2,1)} fusion(f32[6,764,764]{1,2,0:T(8,128)} %get-tuple-element.13, f32[6,764]{1,0:T(8,128)} %get-tuple-element.12, pred[764,764]{0,1:T(8,128)(4,1)} %copy-done, bf16[764,3,6,128]{0,3,2,1:T(8,128)(2,1)S(1)} %bitcast.69), kind=kOutput, calls=%fused_computation.31 | convolution fusion | flops 911152512 | bytes 16963888 | tf_op jit(solution)/shard_map/hqk,khd->qhd/dot_general | solution.py:30
  31.3 0.0 all-gather.5.cloned.1.call-update
  31.3 0.0 all-gather.7.cloned.1.call-start
  31.4 0.7 all-gather.7.cloned.1.call-update
  32.1 0.0 all-reduce.3.cloned.1.call-start
  32.1 0.0 copy-done.3
  32.1 0.2 reduce_window_sum.18
  32.3 0.0 copy-done.6
  32.3 0.1 select_reduce_fusion.1
  32.4 0.1 add_minimum_fusion
  32.5 0.1 min.22
  32.6 0.1 compare_and_fusion
  32.7 0.1 iota_compare_fusion.5
  32.8 38.9 %all-gather.5.cloned.1.call-done = bf16[764,3072]{0,1:T(8,128)(2,1)} async-done(((bf16[764,768]{0,1:T(8,128)(2,1)}), bf16[764,3072]{0,1:T(8,128)(2,1)}) %all-gather.5.cloned.1.call-update) | async-done | bytes 4694032 | tf_op jit(solution)/shard_map/all_gather | solution.py:37
  71.7 168.4 %all-gather.7.cloned.1.call-done = bf16[3072,1536]{1,0:T(8,128)(2,1)} async-done(((bf16[768,1536]{1,0:T(8,128)(2,1)}), bf16[3072,1536]{1,0:T(8,128)(2,1)}) %all-gather.7.cloned.1.call-update) | async-done | bytes 9437200 | tf_op jit(solution)/shard_map/all_gather | solution.py:40
  240.1 12.0 %fusion.4 = bf16[764,1536]{1,0:T(8,128)(2,1)S(1)} fusion(bf16[764,3072]{0,1:T(8,128)(2,1)} %all-gather.5.cloned.1.call-done, bf16[3072,1536]{1,0:T(8,128)(2,1)} %all-gather.7.cloned.1.call-done, bf16[1,764,1536]{2,1,0:T(8,128)(2,1)} %param.11), kind=kOutput, calls=%fused_computation.9 | convolution fusion | flops 7213529088 | bytes 18825216 | tf_op jit(solution)/shard_map/dot_general | solution.py:38
  252.0 0.4 fusion.21
  252.4 13.3 %all-gather.1 = bf16[4,4,1536]{2,1,0:T(4,128)(2,1)S(1)} all-gather(bf16[1,4,1536]{2,1,0:T(4,128)(2,1)S(1)} %fusion.21), channel_id=2, replica_groups=mesh['groups'=2,'dp'=4,'mp'=4] {'dp'}, dimensions={0}, use_global_device_ids=true | all-gather | bytes 61440 | tf_op jit(solution)/shard_map/all_gather | solution.py:57
  265.8 5.1 %fusion.5 = bf16[4,4,3072]{2,1,0:T(4,128)(2,1)S(1)} fusion(bf16[4,4,1536]{2,1,0:T(4,128)(2,1)S(1)} %all-gather.1, bf16[1536,3072]{1,0:T(8,128)(2,1)} %param.13), kind=kOutput, calls=%fused_computation.10 | convolution fusion | flops 151044096 | bytes 9584640 | tf_op jit(solution)/shard_map/abd,dc->abc/dot_general | solution.py:55
  270.9 0.7 copy.35
  271.6 0.0 all-reduce.3.cloned.1.call-update
  271.6 0.0 copy-done.9
  271.6 0.6 dynamic-slice
  272.2 3.8 gather_fusion
  276.0 2.3 gather.13
  278.3 23.2 %all-reduce.3.cloned.1.call-done = bf16[4,4,3072]{2,0,1:T(4,128)(2,1)} async-done(((bf16[4,4,3072]{2,0,1:T(4,128)(2,1)}), bf16[4,4,3072]{2,0,1:T(4,128)(2,1)}) %all-reduce.3.cloned.1.call-update) | async-done | bytes 98320
  301.5 0.0 copy-done.4
  301.5 1.4 fusion.34
  302.9 0.5 broadcast.206
  303.4 0.7 reduce.11
  304.1 0.6 reshape.285
  304.7 4.6 %all-to-all-start.1 = ((bf16[4,2,1536]{2,1,0:T(2,128)(2,1)}), bf16[4,2,1536]{2,1,0:T(2,128)(2,1)S(1)}, u32[]{:S(2)}, u32[]{:S(2)}) async-start(bf16[4,2,1536]{2,1,0:T(2,128)(2,1)} %reshape.285), calls=%async_computation.1 | async-start | bytes 49152 | tf_op jit(solution)/shard_map/all_to_all | solution.py:121
  309.3 1.7 select_select_fusion
  311.1 3.9 %all-to-all-done.1 = bf16[4,2,1536]{2,1,0:T(2,128)(2,1)S(1)} async-done(((bf16[4,2,1536]{2,1,0:T(2,128)(2,1)}), bf16[4,2,1536]{2,1,0:T(2,128)(2,1)S(1)}, u32[]{:S(2)}, u32[]{:S(2)}) %all-to-all-start.1) | async-done | bytes 24608 | tf_op jit(solution)/shard_map/all_to_all | solution.py:121
  315.0 4.5 %all-to-all-start = ((bf16[4,191,1536]{2,1,0:T(8,128)(2,1)}), bf16[4,191,1536]{2,1,0:T(8,128)(2,1)}, u32[]{:S(2)}, u32[]{:S(2)}) async-start(bf16[4,191,1536]{2,1,0:T(8,128)(2,1)} %select_select_fusion), calls=%async_computation | async-start | bytes 4718592 | tf_op jit(solution)/shard_map/all_to_all | solution.py:115
  319.4 0.2 fusion.44
  319.7 0.1 reduce.2
  319.8 0.1 convert_reduce_fusion.2
  319.9 0.1 select_reduce_fusion.2
  320.1 0.7 convert.3
  320.7 50.3 %all-to-all-done = bf16[4,191,1536]{2,1,0:T(8,128)(2,1)} async-done(((bf16[4,191,1536]{2,1,0:T(8,128)(2,1)}), bf16[4,191,1536]{2,1,0:T(8,128)(2,1)}, u32[]{:S(2)}, u32[]{:S(2)}) %all-to-all-start) | async-done | bytes 2347040 | tf_op jit(solution)/shard_map/all_to_all | solution.py:115
  371.1 2.3 reshape.254
  373.4 2.2 gather_fusion.1
  375.6 1.2 bitcast_select_fusion
  (18 shorter events, 0.2 us)
Async XLA Ops:
  7.2 64.5 %all-gather.5.cloned.1.call-start = ((), (), s32[]{:S(2)}) async-start(), calls=%async_computation.2 | async-start | bytes 5898240 | tf_op jit(solution)/shard_map/all_gather | solution.py:37
  11.5 2.4 copy-start.5
  11.5 2.8 copy-start.7
  11.5 2.8 copy-start.8
  11.9 1.4 copy-start.1
  12.0 1.3 copy-start.2
  14.4 8.7 %copy-start = (pred[764,764]{0,1:T(8,128)(4,1)}, pred[764,764]{0,1:T(8,128)(4,1)S(1)}, u32[]{:S(2)}) copy-start(pred[764,764]{0,1:T(8,128)(4,1)S(1)} %broadcast_compare_fusion) | copy-start | bytes 1751092
  31.3 0.8 copy-start.3
  31.3 1.0 copy-start.6
  31.3 208.7 %all-gather.7.cloned.1.call-start = ((), (), s32[]{:S(2)}) async-start(), calls=%async_computation.3 | async-start | bytes 11796480 | tf_op jit(solution)/shard_map/all_gather | solution.py:40
  32.1 269.4 %all-reduce.3.cloned.1.call-start = ((), (), s32[]{:S(2)}) async-start(), calls=%async_computation.4 | async-start | bytes 196608
  265.8 5.8 %copy-start.9 = (u32[32]{0:T(128)S(1)}, u32[32]{0:T(128)}, u32[]{:S(2)}) copy-start(u32[32]{0:T(128)} %constant.81) | copy-start | bytes 388
  276.0 25.5 %copy-start.4 = (f32[3072]{0:T(1024)S(1)}, f32[3072]{0:T(1024)}, u32[]{:S(2)}) copy-start(f32[3072]{0:T(1024)} %param.14) | copy-start | bytes 36868
  304.7 10.2 %all-to-all-start.1 = ((bf16[4,2,1536]{2,1,0:T(2,128)(2,1)}), bf16[4,2,1536]{2,1,0:T(2,128)(2,1)S(1)}, u32[]{:S(2)}, u32[]{:S(2)}) async-start(bf16[4,2,1536]{2,1,0:T(2,128)(2,1)} %reshape.285), calls=%async_computation.1 | async-start | bytes 49152 | tf_op jit(solution)/shard_map/all_to_all | solution.py:121
  315.0 56.1 %all-to-all-start = ((bf16[4,191,1536]{2,1,0:T(8,128)(2,1)}), bf16[4,191,1536]{2,1,0:T(8,128)(2,1)}, u32[]{:S(2)}, u32[]{:S(2)}) async-start(bf16[4,191,1536]{2,1,0:T(8,128)(2,1)} %select_select_fusion), calls=%async_computation | async-start | bytes 4718592 | tf_op jit(solution)/shard_map/all_to_all | solution.py:115
Sparse Core Ops, SparseCore 0:
  31.4 40.2 all-gather.4
  73.3 166.7 all-gather.6
  271.7 29.7 all-reduce.2
where the time goes:
time: 384 us; the launch traced here: 383 us
  waiting for transfers between devices  285 us (74%)
  matrix products  34.4 us (9%)
  local copies, waits for them, and re-layouts  17.7 us (5%)
  between operations  14 us (4%)
  blocking collectives  13.3 us (3%)
  other arithmetic  9.38 us (2%)
  starting transfers between devices  9.2 us (2%)
    all_gather x1, waiting for transfers between devices, project(): lax.all_gather(out_weight, 'dp', axis=0, tiled=True)  168 us
    all_to_all x1, waiting for transfers between devices, on_device(): lax.all_to_all(send_mixed, 'dp', split_axis=0, concat_axis=0, tiled=True)  50.3 us
    all_gather x1, waiting for transfers between devices, project(): gathered = lax.all_gather(heads_local, 'mp', axis=1, tiled=True)  38.9 us
    unnamed x4, waiting for transfers between devices  23.9 us
    all_gather x1, blocking collectives, label_terms(): lax.all_gather(pooled[None], 'dp', axis=0, tiled=True)  13.3 us
    dot_general x1, matrix products, project(): jnp.dot(gathered, lax.all_gather(out_weight, 'dp', axis=0, tiled=True), p...  12 us
    dot_general x1, matrix products, attend(): jnp.einsum('qhd,khd->hqk', queries, key_rows, preferred_element_type=jnp....  8.66 us
    dot_general x1, matrix products, attend(): jnp.einsum('hqk,khd->qhd', weights, split_parts[:, 2], preferred_element_...  8.27 us
  transfers between devices with their start and end apart: 5, of which 5 were waited for; matrix products, arithmetic and copies ran while one was open for 3% of the time, Pallas kernels for 0%

commit v1 on v0

--- a/solution.py
+++ b/solution.py
@@ -34,7 +34,12 @@
 
 
 def project(heads_local, resid_rows, out_weight):
-    gathered = lax.all_gather(heads_local, "mp", axis=1, tiled=True)
+    ring = [heads_local]
+    for hop in range(3):
+        ring.append(lax.ppermute(ring[-1], "mp", [(dev, (dev + 1) % 4) for dev in range(4)]))
+    gathered = jnp.roll(
+        jnp.concatenate(ring[::-1], axis=1), (lax.axis_index("mp") + 1) * ring[0].shape[1], axis=1
+    )
     running = resid_rows.astype(jnp.float32) + jnp.dot(
         gathered,
         lax.all_gather(out_weight, "dp", axis=0, tiled=True),

time: 384 us -> 323 us (0.84)
  waiting for transfers between devices: 285 us -> 212 us
  local copies, waits for them, and re-layouts: 17.7 us -> 27.6 us
    all_gather x1, waiting for transfers between devices: 168 us -> 90.7 us  [project(): lax.all_gather(out_weight, 'dp', axis=0, tiled=True)]
    ppermute x0 -> x3, waiting for transfers between devices: none -> 43 us  [project(): lax.ppermute(ring[-1], 'mp', [(dev, (dev + 1) % 4) for dev in range(4)])]
    all_gather x1 -> x0, waiting for transfers between devices: 38.9 us -> none  [project(): gathered = lax.all_gather(heads_local, 'mp', axis=1, tiled=True)]
    unnamed x24 -> x35, local copies, waits for them, and re-layouts: 5.56 us -> 13.8 us
    unnamed x4 -> x3, waiting for transfers between devices: 23.9 us -> 23.9 us
  transfers between devices with their start and end apart: 5 -> 7, of which waited for: 5 -> 7; matrix products, arithmetic and copies ran while one was open for 3% -> 14% of each run, Pallas kernels for 0% -> 0%
where the time goes in v1:
time: 323 us
  waiting for transfers between devices  212 us (66%)
  matrix products  35.2 us (11%)
  local copies, waits for them, and re-layouts  27.6 us (9%)
  between operations  14.3 us (4%)
  blocking collectives  13.3 us (4%)
  other arithmetic  10.8 us (3%)
  starting transfers between devices  9.65 us (3%)
    all_gather x1, waiting for transfers between devices, project(): lax.all_gather(out_weight, 'dp', axis=0, tiled=True)  90.7 us
    all_to_all x1, waiting for transfers between devices, on_device(): lax.all_to_all(send_mixed, 'dp', split_axis=0, concat_axis=0, tiled=True)  50.3 us
    ppermute x3, waiting for transfers between devices, project(): lax.ppermute(ring[-1], 'mp', [(dev, (dev + 1) % 4) for dev in range(4)])  43 us
    unnamed x3, waiting for transfers between devices  23.9 us
    unnamed x35, local copies, waits for them, and re-layouts  13.8 us
    all_gather x1, blocking collectives, label_terms(): lax.all_gather(pooled[None], 'dp', axis=0, tiled=True)  13.3 us
    dot_general x1, matrix products, project(): jnp.dot(gathered, lax.all_gather(out_weight, 'dp', axis=0, tiled=True), p...  12 us
    dot_general x1, matrix products, attend(): jnp.einsum('hqk,khd->qhd', weights, split_parts[:, 2], preferred_element_...  9.18 us
  transfers between devices with their start and end apart: 7, of which 7 were waited for; matrix products, arithmetic and copies ran while one was open for 14% of the time, Pallas kernels for 0%

profile of v1, /device:TPU:0, one launch (start us, length us, event | category | flops | bytes accessed | tf_op | source)
XLA Modules:
  0.0 322.7 jit_solution(11660341526595513351)
XLA Ops:
  7.2 0.0 all-gather.4.cloned.1.call-start
  7.2 0.7 all-gather.4.cloned.1.call-update
  7.9 0.0 copy-start.6
  7.9 0.0 all-reduce.3.cloned.1.call-start
  8.0 4.3 %copy.31 = bf16[1,764,3,768]{1,3,2,0:T(8,128)(2,1)S(1)} copy(bf16[1,764,3,768]{3,1,2,0:T(8,128)(2,1)} %param.10) | data formatting | bytes 7041024 | tf_op args[0]
  12.3 0.0 copy-start.9
  12.3 0.0 copy-start.10
  12.3 0.4 convert_reduce_fusion.1
  12.7 0.7 fusion.15
  13.5 0.4 broadcast_compare_fusion
  13.9 8.5 %fusion = (f32[6,764]{1,0:T(8,128)}, f32[6,764,764]{1,2,0:T(8,128)}) fusion(pred[764,764]{0,1:T(8,128)(4,1)S(1)} %broadcast_compare_fusion, f32[128]{0:T(128)S(1)} %copy-done.9, f32[764,6]{0,1:T(8,128)S(1)} %add_rsqrt_fusion, f32[764,6]{0,1:T(8,128)S(1)} %get-tuple-element.14, bf16[764,3,6,128]{0,3,2,1:T(8,128)(2,1)S(1)} %bitcast.67, f32[128]{0:T(128)S(1)} %copy-done.10, ...), kind=kOutput, calls=%fused_computation.4 | convolution fusion | flops 912926592 | bytes 17075488 | tf_op jit(solution)/shard_map/qhd,khd->hqk/dot_general | solution.py:24
  22.4 9.2 %fusion.26 = bf16[6,764,128]{1,2,0:T(8,128)(2,1)} fusion(f32[6,764,764]{1,2,0:T(8,128)} %get-tuple-element.13, f32[6,764]{1,0:T(8,128)} %get-tuple-element.12, pred[764,764]{0,1:T(8,128)(4,1)} %copy-done.1, bf16[764,3,6,128]{0,3,2,1:T(8,128)(2,1)S(1)} %bitcast.68), kind=kOutput, calls=%fused_computation.33 | convolution fusion | flops 911152512 | bytes 16963888 | tf_op jit(solution)/shard_map/hqk,khd->qhd/dot_general | solution.py:30
  31.6 0.5 collective-permute-start
  32.1 16.1 %collective-permute-done = bf16[764,768]{0,1:T(8,128)(2,1)S(1)} collective-permute-done((bf16[764,768]{0,1:T(8,128)(2,1)}, bf16[764,768]{0,1:T(8,128)(2,1)S(1)}, u32[]{:S(2)}, u32[]{:S(2)}) %collective-permute-start) | collective-permute-done | bytes 1173536 | tf_op jit(solution)/shard_map/ppermute | solution.py:39
  48.1 0.0 collective-permute-start.1
  48.2 15.6 %collective-permute-done.1 = bf16[764,768]{0,1:T(8,128)(2,1)S(1)} collective-permute-done((bf16[764,768]{0,1:T(8,128)(2,1)S(1)}, bf16[764,768]{0,1:T(8,128)(2,1)S(1)}, u32[]{:S(2)}, u32[]{:S(2)}) %collective-permute-start.1) | collective-permute-done | bytes 1173536 | tf_op jit(solution)/shard_map/ppermute | solution.py:39
  63.8 0.0 collective-permute-start.2
  63.8 0.2 reduce_window_sum.18
  64.0 0.8 select_reduce_fusion.1
  64.8 0.5 fusion.43
  65.3 0.1 copy-done.4
  65.3 0.5 copy-done.7
  65.9 0.1 add_minimum_fusion
  65.9 0.1 min.22
  66.0 0.6 fusion.46
  66.6 0.7 compare_and_fusion
  67.4 0.7 iota_compare_fusion.5
  68.1 11.3 %collective-permute-done.2 = bf16[764,768]{0,1:T(8,128)(2,1)S(1)} collective-permute-done((bf16[764,768]{0,1:T(8,128)(2,1)S(1)}, bf16[764,768]{0,1:T(8,128)(2,1)S(1)}, u32[]{:S(2)}, u32[]{:S(2)}) %collective-permute-start.2) | collective-permute-done | bytes 1173536 | tf_op jit(solution)/shard_map/ppermute | solution.py:39
  79.4 1.1 constant_dynamic-update-slice_fusion.7
  80.5 1.1 constant_dynamic-update-slice_fusion.6
  81.6 1.1 constant_dynamic-update-slice_fusion.5
  82.7 1.1 constant_dynamic-update-slice_fusion.4
  83.8 1.1 constant_dynamic-update-slice_fusion.3
  84.9 1.1 constant_dynamic-update-slice_fusion.2
  86.0 1.1 constant_dynamic-update-slice_fusion.1
  87.1 1.2 constant_dynamic-update-slice_fusion
  88.3 90.7 %all-gather.4.cloned.1.call-done = bf16[3072,1536]{1,0:T(8,128)(2,1)} async-done(((bf16[768,1536]{1,0:T(8,128)(2,1)}), bf16[3072,1536]{1,0:T(8,128)(2,1)}) %all-gather.4.cloned.1.call-update) | async-done | bytes 9437200 | tf_op jit(solution)/shard_map/all_gather | solution.py:45
  179.1 12.0 %fusion.4 = bf16[764,1536]{1,0:T(8,128)(2,1)S(1)} fusion(bf16[3072,1536]{1,0:T(8,128)(2,1)} %all-gather.4.cloned.1.call-done, bf16[764,6144]{0,1:T(8,128)(2,1)} %constant_dynamic-update-slice_fusion, s32[]{:T(128)S(6)} %select_n.74, bf16[1,764,1536]{2,1,0:T(8,128)(2,1)} %param.11), kind=kOutput, calls=%fused_computation.9 | convolution fusion | flops 7213529088 | bytes 18862084 | tf_op jit(solution)/shard_map/dot_general | solution.py:43
  191.1 0.4 fusion.25
  191.5 13.3 %all-gather.1 = bf16[4,4,1536]{2,1,0:T(4,128)(2,1)S(1)} all-gather(bf16[1,4,1536]{2,1,0:T(4,128)(2,1)S(1)} %fusion.25), channel_id=2, replica_groups=mesh['groups'=2,'dp'=4,'mp'=4] {'dp'}, dimensions={0}, use_global_device_ids=true | all-gather | bytes 61440 | tf_op jit(solution)/shard_map/all_gather | solution.py:62
  204.8 5.1 %fusion.7 = bf16[4,4,3072]{2,1,0:T(4,128)(2,1)S(1)} fusion(bf16[4,4,1536]{2,1,0:T(4,128)(2,1)S(1)} %all-gather.1, bf16[1536,3072]{1,0:T(8,128)(2,1)} %param.13), kind=kOutput, calls=%fused_computation.12 | convolution fusion | flops 151044096 | bytes 9584640 | tf_op jit(solution)/shard_map/abd,dc->abc/dot_general | solution.py:60
  209.9 0.7 copy.35
  210.6 0.0 all-reduce.3.cloned.1.call-update
  210.7 0.6 dynamic-slice
  211.2 3.8 %gather_fusion = bf16[764,1536]{1,0:T(8,128)(2,1)} fusion(bf16[764,1536]{1,0:T(8,128)(2,1)S(1)} %fusion.4, s32[1024]{0:T(1024)S(1)} %pad_clamp_fusion.1), kind=kCustom, calls=%fused_computation | custom fusion | bytes 4697072 | tf_op jit(solution)/shard_map/jit(_take)/gather | solution.py:69
  215.1 2.3 gather.13
  217.3 23.2 %all-reduce.3.cloned.1.call-done = bf16[4,4,3072]{2,0,1:T(4,128)(2,1)} async-done(((bf16[4,4,3072]{2,0,1:T(4,128)(2,1)}), bf16[4,4,3072]{2,0,1:T(4,128)(2,1)}) %all-reduce.3.cloned.1.call-update) | async-done | bytes 98320
  240.5 1.4 fusion.38
  242.0 0.5 broadcast.206
  242.5 0.7 reduce.11
  243.1 0.6 reshape.285
  243.8 4.6 %all-to-all-start.1 = ((bf16[4,2,1536]{2,1,0:T(2,128)(2,1)}), bf16[4,2,1536]{2,1,0:T(2,128)(2,1)S(1)}, u32[]{:S(2)}, u32[]{:S(2)}) async-start(bf16[4,2,1536]{2,1,0:T(2,128)(2,1)} %reshape.285), calls=%async_computation.1 | async-start | bytes 49152 | tf_op jit(solution)/shard_map/all_to_all | solution.py:126
  248.4 1.7 select_select_fusion
  250.1 3.9 %all-to-all-done.1 = bf16[4,2,1536]{2,1,0:T(2,128)(2,1)S(1)} async-done(((bf16[4,2,1536]{2,1,0:T(2,128)(2,1)}), bf16[4,2,1536]{2,1,0:T(2,128)(2,1)S(1)}, u32[]{:S(2)}, u32[]{:S(2)}) %all-to-all-start.1) | async-done | bytes 24608 | tf_op jit(solution)/shard_map/all_to_all | solution.py:126
  254.0 4.5 %all-to-all-start = ((bf16[4,191,1536]{2,1,0:T(8,128)(2,1)}), bf16[4,191,1536]{2,1,0:T(8,128)(2,1)}, u32[]{:S(2)}, u32[]{:S(2)}) async-start(bf16[4,191,1536]{2,1,0:T(8,128)(2,1)} %select_select_fusion), calls=%async_computation | async-start | bytes 4718592 | tf_op jit(solution)/shard_map/all_to_all | solution.py:120
  258.5 0.2 fusion.49
  258.7 0.1 reduce.2
  258.9 0.1 convert_reduce_fusion.2
  258.9 0.1 select_reduce_fusion.2
  259.1 0.7 convert.3
  259.8 50.3 %all-to-all-done = bf16[4,191,1536]{2,1,0:T(8,128)(2,1)} async-done(((bf16[4,191,1536]{2,1,0:T(8,128)(2,1)}), bf16[4,191,1536]{2,1,0:T(8,128)(2,1)}, u32[]{:S(2)}, u32[]{:S(2)}) %all-to-all-start) | async-done | bytes 2347040 | tf_op jit(solution)/shard_map/all_to_all | solution.py:120
  310.1 2.3 reshape.254
  312.4 2.2 gather_fusion.1
  314.7 1.2 bitcast_select_fusion
  (33 shorter events, 0.2 us)
Async XLA Ops:
  7.2 171.9 %all-gather.4.cloned.1.call-start = ((), (), s32[]{:S(2)}) async-start(), calls=%async_computation.2 | async-start | bytes 11796480 | tf_op jit(solution)/shard_map/all_gather | solution.py:45
  7.9 4.3 %copy-start.6 = (s32[1,764]{1,0:T(1,128)S(1)}, s32[1,764]{1,0:T(1,128)}, u32[]{:S(2)}) copy-start(s32[1,764]{1,0:T(1,128)} %param.19) | copy-start | bytes 9172
  7.9 232.6 %all-reduce.3.cloned.1.call-start = ((), (), s32[]{:S(2)}) async-start(), calls=%async_computation.3 | async-start | bytes 196608
  12.3 1.6 copy-start.9
  12.3 1.6 copy-start.10
  13.9 8.5 %copy-start.1 = (pred[764,764]{0,1:T(8,128)(4,1)}, pred[764,764]{0,1:T(8,128)(4,1)S(1)}, u32[]{:S(2)}) copy-start(pred[764,764]{0,1:T(8,128)(4,1)S(1)} %broadcast_compare_fusion) | copy-start | bytes 1751092
  22.4 41.4 %copy-start.2 = (s32[4,4]{1,0:T(4,128)S(1)}, s32[4,4]{1,0:T(4,128)}, u32[]{:S(2)}) copy-start(s32[4,4]{1,0:T(4,128)} %param.17) | copy-start | bytes 196
  31.6 16.6 %collective-permute-start = (bf16[764,768]{0,1:T(8,128)(2,1)}, bf16[764,768]{0,1:T(8,128)(2,1)S(1)}, u32[]{:S(2)}, u32[]{:S(2)}) collective-permute-start(bf16[764,768]{0,1:T(8,128)(2,1)} %bitcast.69), channel_id=1, source_target_pairs={{0,1},{1,2},{2,3},{3,0},{4,5},{5,6},{6,7},{7,4},{8,9},{9,10},{10,1... | collective-permute-start | bytes 3520520 | tf_op jit(solution)/shard_map/ppermute | solution.py:39
  48.1 15.6 %collective-permute-start.1 = (bf16[764,768]{0,1:T(8,128)(2,1)S(1)}, bf16[764,768]{0,1:T(8,128)(2,1)S(1)}, u32[]{:S(2)}, u32[]{:S(2)}) collective-permute-start(bf16[764,768]{0,1:T(8,128)(2,1)S(1)} %collective-permute-done), channel_id=1, source_target_pairs={{0,1},{1,2},{2,3},{3,0},{4,5},{5,6},{6,7},{7,4},{8,9},{9,10},{10,1... | collective-permute-start | bytes 3520520 | tf_op jit(solution)/shard_map/ppermute | solution.py:39
  63.8 15.6 %collective-permute-start.2 = (bf16[764,768]{0,1:T(8,128)(2,1)S(1)}, bf16[764,768]{0,1:T(8,128)(2,1)S(1)}, u32[]{:S(2)}, u32[]{:S(2)}) collective-permute-start(bf16[764,768]{0,1:T(8,128)(2,1)S(1)} %collective-permute-done.1), channel_id=1, source_target_pairs={{0,1},{1,2},{2,3},{3,0},{4,5},{5,6},{6,7},{7,4},{8,9},{9,10},{10,1... | collective-permute-start | bytes 3520520 | tf_op jit(solution)/shard_map/ppermute | solution.py:39
  64.7 0.6 copy-start.4
  65.3 0.6 copy-start.7
  80.5 2.2 copy-start
  88.3 102.8 %copy-start.8 = (f32[4]{0:T(128)S(1)}, f32[4]{0:T(128)}, u32[]{:S(2)}) copy-start(f32[4]{0:T(128)} %fusion.46) | copy-start | bytes 52
  204.8 5.8 %copy-start.11 = (u32[32]{0:T(128)S(1)}, u32[32]{0:T(128)}, u32[]{:S(2)}) copy-start(u32[32]{0:T(128)} %constant.105) | copy-start | bytes 388
  215.1 25.5 %copy-start.3 = (f32[3072]{0:T(1024)S(1)}, f32[3072]{0:T(1024)}, u32[]{:S(2)}) copy-start(f32[3072]{0:T(1024)} %param.14) | copy-start | bytes 36868
  243.8 10.2 %all-to-all-start.1 = ((bf16[4,2,1536]{2,1,0:T(2,128)(2,1)}), bf16[4,2,1536]{2,1,0:T(2,128)(2,1)S(1)}, u32[]{:S(2)}, u32[]{:S(2)}) async-start(bf16[4,2,1536]{2,1,0:T(2,128)(2,1)} %reshape.285), calls=%async_computation.1 | async-start | bytes 49152 | tf_op jit(solution)/shard_map/all_to_all | solution.py:126
  250.1 8.4 %copy-start.5 = (s32[4,4]{1,0:T(4,128)S(1)}, s32[4,4]{1,0:T(4,128)}, u32[]{:S(2)}) copy-start(s32[4,4]{1,0:T(4,128)} %copy-done.4) | copy-start | bytes 196
  254.0 56.1 %all-to-all-start = ((bf16[4,191,1536]{2,1,0:T(8,128)(2,1)}), bf16[4,191,1536]{2,1,0:T(8,128)(2,1)}, u32[]{:S(2)}, u32[]{:S(2)}) async-start(bf16[4,191,1536]{2,1,0:T(8,128)(2,1)} %select_select_fusion), calls=%async_computation | async-start | bytes 4718592 | tf_op jit(solution)/shard_map/all_to_all | solution.py:120
Sparse Core Ops, SparseCore 0:
  9.5 169.4 all-gather.3
  210.8 29.7 all-reduce.2
